TPU v7x, 512 devices: a whole 4x4x16 slice. The times are simulated.
512 devices in a mesh: branch: 4 (over y_hi, core), segment: 8 (over y_lo, x), tp: 16 (over z).
Axes of the slice: x: 4, y: 4 (y_hi: 2, y_lo: 2; y = y_hi * 2 + y_lo), z: 16, core: 2. Of those that a mesh axis runs over, the one named last changes fastest.
Arguments:
- rollout: bfloat16 [2304, 8192], P(('branch', 'segment')), may hold values from -6 to 6
- send_rows: int32 [2304], P(('branch', 'segment')), may hold values from 0 to 71, as said below
- seq_lengths: int32 [8, 6], P('segment'), may hold values from 1 to 144, 288 in all within a row
- attn_gain: bfloat16 [4, 8192], P('branch'), may hold values from 0.099609375 to 1.8984375
- w_query: bfloat16 [4, 8192, 8192], P('branch', 'segment', 'tp'), may hold values from -1 to 1
- w_keyval: bfloat16 [4, 8192, 2048], P('branch', 'segment', 'tp'), may hold values from -1 to 1
- head_weight: bfloat16 [4, 8192], P('branch', 'tp'), may hold values from -0.0625 to 0.0625
- head_attn: bfloat16 [4, 8192], P('branch', 'tp'), may hold values from -0.25 to 0.25
Outputs:
- scores: float32 [4, 2304], P(None, ('branch', 'segment'))
Inputs may be any that keep to these rules, and one draw needn't show every extreme that they name: `send_rows`: each aligned block of 72 entries holds every number of 0 to 71 once.
All inputs are finite; a program needn't handle non-finite values.
Results may differ from a plain program's by a relative error of at most 0.006.
Values may be sent and summed in bfloat16 or wider, within the bound.
A program may use at most 128 MiB of HBM per device.

v0:
```python
import math
import jax
import jax.numpy as jnp
from jax import lax
from jax.sharding import PartitionSpec as P

HEAD = 128
HEADS = 64
KV_HEADS = 8
epsilon = 1e-05


def local(rollout, send_rows, seq_lengths, attn_gain, w_query, w_keyval, head_weight, head_attn):
    n_branch = lax.axis_size("branch")
    n_segment = lax.axis_size("segment")
    gen_rows = rollout.shape[0]
    piece_rows = gen_rows // n_segment
    row_width = rollout.shape[1]
    ordered = jnp.take(rollout, send_rows, axis=0).reshape(n_segment, piece_rows, row_width)
    copies = jnp.broadcast_to(ordered[None], (n_branch, n_segment, piece_rows, row_width))
    copies = copies.reshape(n_branch * n_segment, piece_rows, row_width)
    arrived = lax.all_to_all(copies, ("branch", "segment"), split_axis=0, concat_axis=0, tiled=True)
    packed = arrived.reshape(-1, row_width)
    pack_rows = packed.shape[0]
    rows_float = packed.astype(jnp.float32)
    mean_square = jnp.mean(rows_float * rows_float, axis=-1, keepdims=True)
    normed = (
        rows_float * lax.rsqrt(mean_square + epsilon) * attn_gain[0].astype(jnp.float32)
    ).astype(jnp.bfloat16)
    query_acc = jnp.dot(
        normed,
        lax.all_gather(w_query, "segment", axis=1, tiled=True)[0],
        preferred_element_type=jnp.float32,
    )
    keyval_acc = jnp.dot(
        normed,
        lax.all_gather(w_keyval, "segment", axis=1, tiled=True)[0],
        preferred_element_type=jnp.float32,
    )
    queries = query_acc.astype(jnp.bfloat16)
    keyval_part = keyval_acc.astype(jnp.bfloat16)
    keyval = lax.all_gather(keyval_part, "tp", axis=1, tiled=True)
    tp_index = lax.axis_index("tp")
    heads_here = queries.shape[1] // HEAD
    group_size = HEADS // KV_HEADS
    per_group = min(heads_here, group_size)
    group_span = heads_here // per_group
    kv_first = tp_index * heads_here // group_size
    key_rows = lax.dynamic_slice_in_dim(keyval, kv_first * HEAD, group_span * HEAD, 1)
    value_rows = lax.dynamic_slice_in_dim(
        keyval, KV_HEADS * HEAD + kv_first * HEAD, group_span * HEAD, 1
    )
    key_rows = key_rows.reshape(pack_rows, group_span, HEAD)
    value_rows = value_rows.reshape(pack_rows, group_span, HEAD)
    queries = queries.reshape(pack_rows, group_span, per_group, HEAD)
    positions = jnp.arange(pack_rows, dtype=jnp.int32)
    doc_ends = jnp.cumsum(seq_lengths[0])
    doc_ids = jnp.sum((positions[:, None] >= doc_ends[None, :]).astype(jnp.int32), axis=-1)
    visible = (doc_ids[:, None] == doc_ids[None, :]) & (positions[None, :] <= positions[:, None])
    logits = jnp.einsum(
        "qgpc,kgc->gpqk", queries, key_rows, preferred_element_type=jnp.float32
    ) / math.sqrt(HEAD)
    logits = jnp.where(visible[None, None], logits, -1e30)
    row_max = jnp.max(logits, axis=-1, keepdims=True)
    expo = jnp.exp(logits - row_max)
    probabilities = (expo / jnp.sum(expo, axis=-1, keepdims=True)).astype(jnp.bfloat16)
    attended = jnp.einsum(
        "gpqk,kgc->qgpc", probabilities, value_rows, preferred_element_type=jnp.float32
    )
    attended = attended.reshape(pack_rows, heads_here * HEAD)
    slice_width = head_weight.shape[1]
    own_columns = lax.dynamic_slice_in_dim(packed, tp_index * slice_width, slice_width, 1)
    direct = jnp.dot(own_columns, head_weight[0], preferred_element_type=jnp.float32)
    through = jnp.dot(attended, head_attn[0].astype(jnp.float32), precision=lax.Precision.HIGHEST)
    totals = lax.psum(direct + through, "tp")
    outgoing = totals.reshape(n_branch * n_segment, piece_rows)
    incoming = lax.all_to_all(
        outgoing, ("branch", "segment"), split_axis=0, concat_axis=0, tiled=True
    )
    incoming = incoming.reshape(n_branch, n_segment * piece_rows)
    scores = jnp.zeros((n_branch, gen_rows), jnp.float32).at[:, send_rows].set(incoming)
    return scores


def solution(mesh):
    return jax.shard_map(
        local,
        mesh=mesh,
        in_specs=(
            P(("branch", "segment"), None),
            P(("branch", "segment")),
            P("segment", None),
            P("branch", None),
            P("branch", "segment", "tp"),
            P("branch", "segment", "tp"),
            P("branch", "tp"),
            P("branch", "tp"),
        ),
        out_specs=P(None, ("branch", "segment")),
        check_vma=False,
    )
```

profile of v0, /device:TPU:1, one launch (start us, length us, event | category | flops | bytes accessed | tf_op | source)
XLA Modules:
  0.0 387.5 jit_solution(12303742169167186144)
XLA Ops:
  6.5 0.7 all-gather.4.cloned.1.call-update
  7.3 0.7 all-gather.8.cloned.1.call-update
  8.0 0.7 compare_select_fusion
  8.7 2.4 gather_fusion
  11.1 1.8 gather.7
  13.3 4.4 %broadcast_in_dim.51 = bf16[4,8,9,8192]{3,2,1,0:T(8,128)(2,1)} broadcast(bf16[8,9,8192]{2,1,0:T(8,128)(2,1)S(1)} %broadcast_select_fusion), dimensions={1,2,3} | broadcast | bytes 5898240 | tf_op jit(solution)/shard_map/broadcast_in_dim | solution.py:20
  17.7 11.6 %all-to-all-start = ((bf16[32,9,8192]{2,1,0:T(8,128)(2,1)}), bf16[32,9,8192]{2,1,0:T(8,128)(2,1)}, u32[]{:S(2)}, u32[]{:S(2)}) async-start(bf16[32,9,8192]{2,1,0:T(8,128)(2,1)} %bitcast.58), calls=%async_computation | async-start | bytes 16777216 | tf_op jit(solution)/shard_map/all_to_all | solution.py:22
  29.6 144.8 %all-to-all-done = bf16[32,9,8192]{2,1,0:T(8,128)(2,1)} async-done(((bf16[32,9,8192]{2,1,0:T(8,128)(2,1)}), bf16[32,9,8192]{2,1,0:T(8,128)(2,1)}, u32[]{:S(2)}, u32[]{:S(2)}) %all-to-all-start) | async-done | bytes 4718624 | tf_op jit(solution)/shard_map/all_to_all | solution.py:22
  174.5 5.4 %fusion = f32[32,9]{1,0:T(8,128)S(1)} fusion(bf16[32,9,8192]{2,1,0:T(8,128)(2,1)} %all-to-all-done), kind=kLoop, calls=%fused_computation.4 | loop fusion | flops 7077600 | bytes 4719744 | tf_op jit(solution)/shard_map/reduce_sum | solution.py:26
  179.9 9.9 %fusion.2 = bf16[32,9,8192]{2,1,0:T(8,128)(2,1)} fusion(bf16[32,9,8192]{2,1,0:T(8,128)(2,1)} %all-to-all-done, f32[8192]{0:T(1024)S(1)} %bitcast.60, f32[32,9]{1,0:T(8,128)S(1)} %add_rsqrt_fusion), kind=kLoop, calls=%fused_computation.6 | loop fusion | flops 9437184 | bytes 9471104 | tf_op jit(solution)/shard_map/convert_element_type | solution.py:29
  189.9 6.9 %convert_element_type.30 = bf16[288,8192]{1,0:T(8,128)(2,1)} reshape(bf16[32,9,8192]{2,1,0:T(8,128)(2,1)} %fusion.2) | data formatting | bytes 9437184 | tf_op jit(solution)/shard_map/convert_element_type | solution.py:29
  196.8 5.1 %fusion.14 = bf16[288,128]{1,0:T(8,128)(2,1)} fusion(bf16[288,8192]{1,0:T(8,128)(2,1)} %convert_element_type.30, bf16[1,8192,128]{2,1,0:T(8,128)(2,1)} %all-gather.4.cloned.1.call-done), kind=kOutput, calls=%fused_computation.19 | convolution fusion | flops 604016640 | bytes 6889472 | tf_op jit(solution)/shard_map/dot_general | solution.py:35
  202.4 6.9 %reshape.163 = bf16[288,8192]{1,0:T(8,128)(2,1)} reshape(bf16[32,9,8192]{2,1,0:T(8,128)(2,1)} %all-to-all-done) | data formatting | bytes 9437184 | tf_op jit(solution)/shard_map/reshape | solution.py:23
  209.3 1.2 convolution_reduce_fusion.1
  210.5 17.9 %all-gather.8.cloned.1.call-done = bf16[1,8192,512]{2,1,0:T(8,128)(2,1)} async-done(((bf16[1,1024,512]{2,1,0:T(8,128)(2,1)}), bf16[1,8192,512]{2,1,0:T(8,128)(2,1)}) %all-gather.8.cloned.1.call-update) | async-done | bytes 8388624 | tf_op jit(solution)/shard_map/all_gather | solution.py:32
  228.4 7.4 %fusion.11 = bf16[36,4,8,128]{3,2,1,0:T(8,128)(2,1)S(1)} fusion(bf16[288,8192]{1,0:T(8,128)(2,1)} %convert_element_type.30, bf16[1,8192,512]{2,1,0:T(8,128)(2,1)} %all-gather.8.cloned.1.call-done), kind=kOutput, calls=%fused_computation.18 | convolution fusion | flops 2416066560 | bytes 13402112 | tf_op jit(solution)/shard_map/dot_general | solution.py:30
  235.8 58.6 %all-gather.6.cloned.1.call-done = bf16[288,2048]{1,0:T(8,128)(2,1)} async-done(((bf16[288,128]{1,0:T(8,128)(2,1)}), bf16[288,2048]{1,0:T(8,128)(2,1)}) %all-gather.6.cloned.1.call-update) | async-done | bytes 1179664 | tf_op jit(solution)/shard_map/all_gather | solution.py:42
  294.4 1.4 fusion.35
  296.1 1.5 convolution_bitcast_fusion
  298.5 40.6 %psum.7 = f32[32,1,9]{2,0,1:T(8,128)S(1)} all-reduce(f32[32,1,9]{2,0,1:T(8,128)S(1)} %all_to_all.10), channel_id=1, replica_groups=mesh['branch'=4,'segment'=8,'tp'=16] {'tp'}, use_global_device_ids=true, to_apply=%region_5.6 | all-reduce | flops 288 | bytes 2304 | tf_op jit(solution)/shard_map/psum | solution.py:75
  339.0 39.1 %all_to_all.14 = f32[32,1,9]{2,1,0:T(1,128)S(1)} all-to-all(f32[32,1,9]{2,1,0:T(1,128)S(1)} %bitcast.61), channel_id=1, replica_groups=mesh['branch'=4,'segment'=8,'tp'=16] {'branch','segment'}, dimensions={0} | all-to-all | bytes 2304 | tf_op jit(solution)/shard_map/all_to_all | solution.py:77
  378.7 0.7 reduce.10
  379.6 0.7 scatter_custom_fusion
  380.3 0.7 copy.28
  (34 shorter events, 3.0 us)
Async XLA Ops:
  6.5 2.1 copy-start
  6.5 190.3 %all-gather.4.cloned.1.call-start = ((), (), s32[]{:S(2)}) async-start(), calls=%async_computation.2 | async-start | bytes 2359296 | tf_op jit(solution)/shard_map/all_gather | solution.py:37
  7.3 221.2 %all-gather.8.cloned.1.call-start = ((), (), s32[]{:S(2)}) async-start(), calls=%async_computation.4 | async-start | bytes 9437184 | tf_op jit(solution)/shard_map/all_gather | solution.py:32
  11.1 1.8 copy-start.4
  17.7 11.9 %copy-start.1 = (bf16[1,8192]{1,0:T(2,128)(2,1)S(1)}, bf16[1,8192]{1,0:T(2,128)(2,1)}, u32[]{:S(2)}) copy-start(bf16[1,8192]{1,0:T(2,128)(2,1)} %param.11) | copy-start | bytes 49156
  17.7 156.7 %all-to-all-start = ((bf16[32,9,8192]{2,1,0:T(8,128)(2,1)}), bf16[32,9,8192]{2,1,0:T(8,128)(2,1)}, u32[]{:S(2)}, u32[]{:S(2)}) async-start(bf16[32,9,8192]{2,1,0:T(8,128)(2,1)} %bitcast.58), calls=%async_computation | async-start | bytes 16777216 | tf_op jit(solution)/shard_map/all_to_all | solution.py:22
  29.4 265.0 %all-gather.6.cloned.1.call-start = ((), (), s32[]{:S(2)}) async-start(), calls=%async_computation.3 | async-start | bytes 1253376 | tf_op jit(solution)/shard_map/all_gather | solution.py:42
  196.8 5.2 %copy-start.5 = (s32[1,6]{1,0:T(1,128)S(1)}, s32[1,6]{1,0:T(1,128)}, u32[]{:S(2)}) copy-start(s32[1,6]{1,0:T(1,128)} %param.10) | copy-start | bytes 76
  202.4 6.9 %copy-start.2 = (bf16[1,512]{1,0:T(2,128)(2,1)S(1)}, bf16[1,512]{1,0:T(2,128)(2,1)}, u32[]{:S(2)}) copy-start(bf16[1,512]{1,0:T(2,128)(2,1)} %param.14) | copy-start | bytes 3076
  296.1 1.9 copy-start.3
Sparse Core Ops, SparseCore 0:
  9.4 92.1 all-gather.3
  103.7 124.6 all-gather.7
  230.4 63.9 all-gather.5
where the time goes:
time: 388 us; the launch traced here: 387 us
  waiting for transfers between devices  223 us (57%)
  blocking collectives  79.7 us (21%)
  local copies, waits for them, and re-layouts  25.2 us (6%)
  other arithmetic  17.7 us (5%)
  matrix products  17 us (4%)
  between operations  13.3 us (3%)
  starting transfers between devices  11.9 us (3%)
    all_to_all x1, waiting for transfers between devices, local(): lax.all_to_all(copies, ('branch', 'segment'), split_axis=0, concat_axis=0...  145 us
    all_gather x1, waiting for transfers between devices, local(): keyval = lax.all_gather(keyval_part, 'tp', axis=1, tiled=True)  58.6 us
    psum x1, blocking collectives, local(): totals = lax.psum(direct + through, 'tp')  40.6 us
    all_to_all x1, blocking collectives, local(): lax.all_to_all(outgoing, ('branch', 'segment'), split_axis=0, concat_axis...  39.1 us
    all_gather x1, waiting for transfers between devices, local(): lax.all_gather(w_query, 'segment', axis=1, tiled=True)[0]  17.9 us
    all_to_all x1, starting transfers between devices, local(): lax.all_to_all(copies, ('branch', 'segment'), split_axis=0, concat_axis=0...  11.6 us
    convert_element_type x1, other arithmetic, local(): normed = (rows_float * lax.rsqrt(mean_square + epsilon) * attn_gain[0].as...  9.94 us
  transfers between devices with their start and end apart: 4, of which 3 were waited for; matrix products, arithmetic and copies ran while one was open for 14% of the time, Pallas kernels for 0%

commit v1 on v0

--- a/solution.py
+++ b/solution.py
@@ -39,7 +39,12 @@
     )
     queries = query_acc.astype(jnp.bfloat16)
     keyval_part = keyval_acc.astype(jnp.bfloat16)
-    keyval = lax.all_gather(keyval_part, "tp", axis=1, tiled=True)
+    ring = [keyval_part]
+    for hop in range(15):
+        ring.append(lax.ppermute(ring[-1], "tp", [(dev, (dev + 1) % 16) for dev in range(16)]))
+    keyval = jnp.roll(
+        jnp.concatenate(ring[::-1], axis=1), (lax.axis_index("tp") + 1) * ring[0].shape[1], axis=1
+    )
     tp_index = lax.axis_index("tp")
     heads_here = queries.shape[1] // HEAD
     group_size = HEADS // KV_HEADS

time: 388 us -> 433 us (1.12)
  starting transfers between devices: 11.9 us -> 40.5 us
  local copies, waits for them, and re-layouts: 25.2 us -> 46 us
  waiting for transfers between devices: 223 us -> 215 us
    ppermute x0 -> x15, waiting for transfers between devices: none -> 67.3 us  [local(): lax.ppermute(ring[-1], 'tp', [(dev, (dev + 1) % 16) for dev in range(16)])]
    all_gather x1 -> x0, waiting for transfers between devices: 58.6 us -> none  [local(): keyval = lax.all_gather(keyval_part, 'tp', axis=1, tiled=True)]
    ppermute x0 -> x15, starting transfers between devices: none -> 28.8 us  [local(): lax.ppermute(ring[-1], 'tp', [(dev, (dev + 1) % 16) for dev in range(16)])]
    unnamed x12 -> x41, local copies, waits for them, and re-layouts: 0.03 us -> 20.2 us
    all_gather x1, waiting for transfers between devices: 17.9 us -> 0.01 us  [local(): lax.all_gather(w_query, 'segment', axis=1, tiled=True)[0]]
  transfers between devices with their start and end apart: 4 -> 18, of which waited for: 3 -> 15; matrix products, arithmetic and copies ran while one was open for 14% -> 15% of each run, Pallas kernels for 0% -> 0%
where the time goes in v1:
time: 433 us; the launch traced here: 432 us
  waiting for transfers between devices  215 us (50%)
  blocking collectives  81 us (19%)
  local copies, waits for them, and re-layouts  46 us (11%)
  starting transfers between devices  40.5 us (9%)
  other arithmetic  18.4 us (4%)
  matrix products  16.4 us (4%)
  between operations  13.8 us (3%)
    all_to_all x1, waiting for transfers between devices, local(): lax.all_to_all(copies, ('branch', 'segment'), split_axis=0, concat_axis=0...  147 us
    ppermute x15, waiting for transfers between devices, local(): lax.ppermute(ring[-1], 'tp', [(dev, (dev + 1) % 16) for dev in range(16)])  67.3 us
    all_to_all x1, blocking collectives, local(): lax.all_to_all(outgoing, ('branch', 'segment'), split_axis=0, concat_axis...  40.7 us
    psum x1, blocking collectives, local(): totals = lax.psum(direct + through, 'tp')  40.3 us
    ppermute x15, starting transfers between devices, local(): lax.ppermute(ring[-1], 'tp', [(dev, (dev + 1) % 16) for dev in range(16)])  28.8 us
    unnamed x41, local copies, waits for them, and re-layouts  20.2 us
    all_to_all x1, starting transfers between devices, local(): lax.all_to_all(copies, ('branch', 'segment'), split_axis=0, concat_axis=0...  11.6 us
    convert_element_type x1, other arithmetic, local(): normed = (rows_float * lax.rsqrt(mean_square + epsilon) * attn_gain[0].as...  9.93 us
  transfers between devices with their start and end apart: 18, of which 15 were waited for; matrix products, arithmetic and copies ran while one was open for 15% of the time, Pallas kernels for 0%

profile of v1, /device:TPU:1, one launch (start us, length us, event | category | flops | bytes accessed | tf_op | source)
XLA Modules:
  0.0 431.5 jit_solution(10188058841139980493)
XLA Ops:
  14.0 4.4 %broadcast_in_dim.51 = bf16[4,8,9,8192]{3,2,1,0:T(8,128)(2,1)} broadcast(bf16[8,9,8192]{2,1,0:T(8,128)(2,1)S(1)} %broadcast_select_fusion), dimensions={1,2,3} | broadcast | bytes 5898240 | tf_op jit(solution)/shard_map/broadcast_in_dim | solution.py:20
  18.4 11.6 %all-to-all-start = ((bf16[32,9,8192]{2,1,0:T(8,128)(2,1)}), bf16[32,9,8192]{2,1,0:T(8,128)(2,1)}, u32[]{:S(2)}, u32[]{:S(2)}) async-start(bf16[32,9,8192]{2,1,0:T(8,128)(2,1)} %bitcast.58), calls=%async_computation | async-start | bytes 16777216 | tf_op jit(solution)/shard_map/all_to_all | solution.py:22
  30.1 146.7 %all-to-all-done = bf16[32,9,8192]{2,1,0:T(8,128)(2,1)} async-done(((bf16[32,9,8192]{2,1,0:T(8,128)(2,1)}), bf16[32,9,8192]{2,1,0:T(8,128)(2,1)}, u32[]{:S(2)}, u32[]{:S(2)}) %all-to-all-start) | async-done | bytes 4718624 | tf_op jit(solution)/shard_map/all_to_all | solution.py:22
  176.8 5.4 %fusion = f32[32,9]{1,0:T(8,128)S(1)} fusion(bf16[32,9,8192]{2,1,0:T(8,128)(2,1)} %all-to-all-done), kind=kLoop, calls=%fused_computation.4 | loop fusion | flops 7077600 | bytes 4719744 | tf_op jit(solution)/shard_map/reduce_sum | solution.py:26
  182.3 9.9 %fusion.2 = bf16[32,9,8192]{2,1,0:T(8,128)(2,1)} fusion(bf16[32,9,8192]{2,1,0:T(8,128)(2,1)} %all-to-all-done, f32[8192]{0:T(1024)S(1)} %bitcast.60, f32[32,9]{1,0:T(8,128)S(1)} %add_rsqrt_fusion), kind=kLoop, calls=%fused_computation.6 | loop fusion | flops 9437184 | bytes 9471104 | tf_op jit(solution)/shard_map/convert_element_type | solution.py:29
  192.2 7.0 %convert_element_type.30 = bf16[288,8192]{1,0:T(8,128)(2,1)} reshape(bf16[32,9,8192]{2,1,0:T(8,128)(2,1)} %fusion.2) | data formatting | bytes 9437184 | tf_op jit(solution)/shard_map/convert_element_type | solution.py:29
  199.2 4.5 %fusion.14 = bf16[288,128]{1,0:T(8,128)(2,1)S(1)} fusion(bf16[288,8192]{1,0:T(8,128)(2,1)} %convert_element_type.30, bf16[1,8192,128]{2,1,0:T(8,128)(2,1)} %all-gather.3.cloned.1.call-done), kind=kOutput, calls=%fused_computation.19 | convolution fusion | flops 604016640 | bytes 6889472 | tf_op jit(solution)/shard_map/dot_general | solution.py:35
  205.6 10.9 %collective-permute-done = bf16[288,128]{1,0:T(8,128)(2,1)S(1)} collective-permute-done((bf16[288,128]{1,0:T(8,128)(2,1)S(1)}, bf16[288,128]{1,0:T(8,128)(2,1)S(1)}, u32[]{:S(2)}, u32[]{:S(2)}) %collective-permute-start) | collective-permute-done | bytes 73760 | tf_op jit(solution)/shard_map/ppermute | solution.py:44
  218.5 4.8 %collective-permute-done.1 = bf16[288,128]{1,0:T(8,128)(2,1)S(1)} collective-permute-done((bf16[288,128]{1,0:T(8,128)(2,1)S(1)}, bf16[288,128]{1,0:T(8,128)(2,1)S(1)}, u32[]{:S(2)}, u32[]{:S(2)}) %collective-permute-start.1) | collective-permute-done | bytes 73760 | tf_op jit(solution)/shard_map/ppermute | solution.py:44
  225.2 4.4 %collective-permute-done.2 = bf16[288,128]{1,0:T(8,128)(2,1)S(1)} collective-permute-done((bf16[288,128]{1,0:T(8,128)(2,1)S(1)}, bf16[288,128]{1,0:T(8,128)(2,1)S(1)}, u32[]{:S(2)}, u32[]{:S(2)}) %collective-permute-start.2) | collective-permute-done | bytes 73760 | tf_op jit(solution)/shard_map/ppermute | solution.py:44
  231.5 4.4 %collective-permute-done.3 = bf16[288,128]{1,0:T(8,128)(2,1)S(1)} collective-permute-done((bf16[288,128]{1,0:T(8,128)(2,1)S(1)}, bf16[288,128]{1,0:T(8,128)(2,1)S(1)}, u32[]{:S(2)}, u32[]{:S(2)}) %collective-permute-start.3) | collective-permute-done | bytes 73760 | tf_op jit(solution)/shard_map/ppermute | solution.py:44
  237.8 4.4 %collective-permute-done.4 = bf16[288,128]{1,0:T(8,128)(2,1)S(1)} collective-permute-done((bf16[288,128]{1,0:T(8,128)(2,1)S(1)}, bf16[288,128]{1,0:T(8,128)(2,1)S(1)}, u32[]{:S(2)}, u32[]{:S(2)}) %collective-permute-start.4) | collective-permute-done | bytes 73760 | tf_op jit(solution)/shard_map/ppermute | solution.py:44
  244.1 4.4 %collective-permute-done.5 = bf16[288,128]{1,0:T(8,128)(2,1)S(1)} collective-permute-done((bf16[288,128]{1,0:T(8,128)(2,1)S(1)}, bf16[288,128]{1,0:T(8,128)(2,1)S(1)}, u32[]{:S(2)}, u32[]{:S(2)}) %collective-permute-start.5) | collective-permute-done | bytes 73760 | tf_op jit(solution)/shard_map/ppermute | solution.py:44
  250.4 4.7 %collective-permute-done.6 = bf16[288,128]{1,0:T(8,128)(2,1)S(1)} collective-permute-done((bf16[288,128]{1,0:T(8,128)(2,1)S(1)}, bf16[288,128]{1,0:T(8,128)(2,1)S(1)}, u32[]{:S(2)}, u32[]{:S(2)}) %collective-permute-start.6) | collective-permute-done | bytes 73760 | tf_op jit(solution)/shard_map/ppermute | solution.py:44
  256.9 4.8 %collective-permute-done.7 = bf16[288,128]{1,0:T(8,128)(2,1)S(1)} collective-permute-done((bf16[288,128]{1,0:T(8,128)(2,1)S(1)}, bf16[288,128]{1,0:T(8,128)(2,1)S(1)}, u32[]{:S(2)}, u32[]{:S(2)}) %collective-permute-start.7) | collective-permute-done | bytes 73760 | tf_op jit(solution)/shard_map/ppermute | solution.py:44
  263.7 4.4 %collective-permute-done.8 = bf16[288,128]{1,0:T(8,128)(2,1)S(1)} collective-permute-done((bf16[288,128]{1,0:T(8,128)(2,1)S(1)}, bf16[288,128]{1,0:T(8,128)(2,1)S(1)}, u32[]{:S(2)}, u32[]{:S(2)}) %collective-permute-start.8) | collective-permute-done | bytes 73760 | tf_op jit(solution)/shard_map/ppermute | solution.py:44
  270.0 4.4 %collective-permute-done.9 = bf16[288,128]{1,0:T(8,128)(2,1)S(1)} collective-permute-done((bf16[288,128]{1,0:T(8,128)(2,1)S(1)}, bf16[288,128]{1,0:T(8,128)(2,1)S(1)}, u32[]{:S(2)}, u32[]{:S(2)}) %collective-permute-start.9) | collective-permute-done | bytes 73760 | tf_op jit(solution)/shard_map/ppermute | solution.py:44
  276.3 4.4 %collective-permute-done.10 = bf16[288,128]{1,0:T(8,128)(2,1)S(1)} collective-permute-done((bf16[288,128]{1,0:T(8,128)(2,1)S(1)}, bf16[288,128]{1,0:T(8,128)(2,1)S(1)}, u32[]{:S(2)}, u32[]{:S(2)}) %collective-permute-start.10) | collective-permute-done | bytes 73760 | tf_op jit(solution)/shard_map/ppermute | solution.py:44
  282.7 4.2 collective-permute-done.11
  288.9 4.3 collective-permute-done.12
  295.3 6.9 %reshape.163 = bf16[288,8192]{1,0:T(8,128)(2,1)} reshape(bf16[32,9,8192]{2,1,0:T(8,128)(2,1)} %all-to-all-done) | data formatting | bytes 9437184 | tf_op jit(solution)/shard_map/reshape | solution.py:23
  329.3 7.4 %fusion.11 = bf16[36,4,8,128]{3,2,1,0:T(8,128)(2,1)S(1)} fusion(bf16[288,8192]{1,0:T(8,128)(2,1)} %convert_element_type.30, bf16[1,8192,512]{2,1,0:T(8,128)(2,1)} %all-gather.5.cloned.1.call-done), kind=kOutput, calls=%fused_computation.18 | convolution fusion | flops 2416066560 | bytes 13402112 | tf_op jit(solution)/shard_map/dot_general | solution.py:30
  340.9 40.3 %psum.7 = f32[32,1,9]{2,0,1:T(8,128)S(1)} all-reduce(f32[32,1,9]{2,0,1:T(8,128)S(1)} %all_to_all.10), channel_id=1, replica_groups=mesh['branch'=4,'segment'=8,'tp'=16] {'tp'}, use_global_device_ids=true, to_apply=%region_5.6 | all-reduce | flops 288 | bytes 2304 | tf_op jit(solution)/shard_map/psum | solution.py:80
  381.3 40.7 %all_to_all.14 = f32[32,1,9]{2,1,0:T(1,128)S(1)} all-to-all(f32[32,1,9]{2,1,0:T(1,128)S(1)} %bitcast.61), channel_id=1, replica_groups=mesh['branch'=4,'segment'=8,'tp'=16] {'branch','segment'}, dimensions={0} | all-to-all | bytes 2304 | tf_op jit(solution)/shard_map/all_to_all | solution.py:82
  (91 shorter events, 68.6 us)
Async XLA Ops:
  6.5 2.8 copy-start
  6.5 192.7 %all-gather.3.cloned.1.call-start = ((), (), s32[]{:S(2)}) async-start(), calls=%async_computation.2 | async-start | bytes 2359296 | tf_op jit(solution)/shard_map/all_gather | solution.py:37
  7.3 322.1 %all-gather.5.cloned.1.call-start = ((), (), s32[]{:S(2)}) async-start(), calls=%async_computation.3 | async-start | bytes 9437184 | tf_op jit(solution)/shard_map/all_gather | solution.py:32
  18.4 11.6 %copy-start.1 = (bf16[1,8192]{1,0:T(2,128)(2,1)S(1)}, bf16[1,8192]{1,0:T(2,128)(2,1)}, u32[]{:S(2)}) copy-start(bf16[1,8192]{1,0:T(2,128)(2,1)} %param.11) | copy-start | bytes 49156
  18.4 158.4 %all-to-all-start = ((bf16[32,9,8192]{2,1,0:T(8,128)(2,1)}), bf16[32,9,8192]{2,1,0:T(8,128)(2,1)}, u32[]{:S(2)}, u32[]{:S(2)}) async-start(bf16[32,9,8192]{2,1,0:T(8,128)(2,1)} %bitcast.58), calls=%async_computation | async-start | bytes 16777216 | tf_op jit(solution)/shard_map/all_to_all | solution.py:22
  199.2 83.3 %copy-start.4 = (s32[1,6]{1,0:T(1,128)S(1)}, s32[1,6]{1,0:T(1,128)}, u32[]{:S(2)}) copy-start(s32[1,6]{1,0:T(1,128)} %param.10) | copy-start | bytes 76
  203.7 12.9 %collective-permute-start = (bf16[288,128]{1,0:T(8,128)(2,1)S(1)}, bf16[288,128]{1,0:T(8,128)(2,1)S(1)}, u32[]{:S(2)}, u32[]{:S(2)}) collective-permute-start(bf16[288,128]{1,0:T(8,128)(2,1)S(1)} %fusion.14), channel_id=1, source_target_pairs={{0,1},{1,2},{2,3},{3,4},{4,5},{5,6},{6,7},{7,8},{8,9},{9,10},{10,1... | collective-permute-start | bytes 221192 | tf_op jit(solution)/shard_map/ppermute | solution.py:44
  216.6 6.7 %collective-permute-start.1 = (bf16[288,128]{1,0:T(8,128)(2,1)S(1)}, bf16[288,128]{1,0:T(8,128)(2,1)S(1)}, u32[]{:S(2)}, u32[]{:S(2)}) collective-permute-start(bf16[288,128]{1,0:T(8,128)(2,1)S(1)} %collective-permute-done), channel_id=1, source_target_pairs={{0,1},{1,2},{2,3},{3,4},{4,5},{5,6},{6,7},{7,8},{8,9},{9,10},{10,1... | collective-permute-start | bytes 221192 | tf_op jit(solution)/shard_map/ppermute | solution.py:44
  223.3 6.3 %collective-permute-start.2 = (bf16[288,128]{1,0:T(8,128)(2,1)S(1)}, bf16[288,128]{1,0:T(8,128)(2,1)S(1)}, u32[]{:S(2)}, u32[]{:S(2)}) collective-permute-start(bf16[288,128]{1,0:T(8,128)(2,1)S(1)} %collective-permute-done.1), channel_id=1, source_target_pairs={{0,1},{1,2},{2,3},{3,4},{4,5},{5,6},{6,7},{7,8},{8,9},{9,10},{10,1... | collective-permute-start | bytes 221192 | tf_op jit(solution)/shard_map/ppermute | solution.py:44
  229.6 6.3 %collective-permute-start.3 = (bf16[288,128]{1,0:T(8,128)(2,1)S(1)}, bf16[288,128]{1,0:T(8,128)(2,1)S(1)}, u32[]{:S(2)}, u32[]{:S(2)}) collective-permute-start(bf16[288,128]{1,0:T(8,128)(2,1)S(1)} %collective-permute-done.2), channel_id=1, source_target_pairs={{0,1},{1,2},{2,3},{3,4},{4,5},{5,6},{6,7},{7,8},{8,9},{9,10},{10,1... | collective-permute-start | bytes 221192 | tf_op jit(solution)/shard_map/ppermute | solution.py:44
  235.9 6.3 %collective-permute-start.4 = (bf16[288,128]{1,0:T(8,128)(2,1)S(1)}, bf16[288,128]{1,0:T(8,128)(2,1)S(1)}, u32[]{:S(2)}, u32[]{:S(2)}) collective-permute-start(bf16[288,128]{1,0:T(8,128)(2,1)S(1)} %collective-permute-done.3), channel_id=1, source_target_pairs={{0,1},{1,2},{2,3},{3,4},{4,5},{5,6},{6,7},{7,8},{8,9},{9,10},{10,1... | collective-permute-start | bytes 221192 | tf_op jit(solution)/shard_map/ppermute | solution.py:44
  242.2 6.3 %collective-permute-start.5 = (bf16[288,128]{1,0:T(8,128)(2,1)S(1)}, bf16[288,128]{1,0:T(8,128)(2,1)S(1)}, u32[]{:S(2)}, u32[]{:S(2)}) collective-permute-start(bf16[288,128]{1,0:T(8,128)(2,1)S(1)} %collective-permute-done.4), channel_id=1, source_target_pairs={{0,1},{1,2},{2,3},{3,4},{4,5},{5,6},{6,7},{7,8},{8,9},{9,10},{10,1... | collective-permute-start | bytes 221192 | tf_op jit(solution)/shard_map/ppermute | solution.py:44
  248.5 6.6 %collective-permute-start.6 = (bf16[288,128]{1,0:T(8,128)(2,1)S(1)}, bf16[288,128]{1,0:T(8,128)(2,1)S(1)}, u32[]{:S(2)}, u32[]{:S(2)}) collective-permute-start(bf16[288,128]{1,0:T(8,128)(2,1)S(1)} %collective-permute-done.5), channel_id=1, source_target_pairs={{0,1},{1,2},{2,3},{3,4},{4,5},{5,6},{6,7},{7,8},{8,9},{9,10},{10,1... | collective-permute-start | bytes 221192 | tf_op jit(solution)/shard_map/ppermute | solution.py:44
  255.0 6.7 %collective-permute-start.7 = (bf16[288,128]{1,0:T(8,128)(2,1)S(1)}, bf16[288,128]{1,0:T(8,128)(2,1)S(1)}, u32[]{:S(2)}, u32[]{:S(2)}) collective-permute-start(bf16[288,128]{1,0:T(8,128)(2,1)S(1)} %collective-permute-done.6), channel_id=1, source_target_pairs={{0,1},{1,2},{2,3},{3,4},{4,5},{5,6},{6,7},{7,8},{8,9},{9,10},{10,1... | collective-permute-start | bytes 221192 | tf_op jit(solution)/shard_map/ppermute | solution.py:44
  261.7 6.3 %collective-permute-start.8 = (bf16[288,128]{1,0:T(8,128)(2,1)S(1)}, bf16[288,128]{1,0:T(8,128)(2,1)S(1)}, u32[]{:S(2)}, u32[]{:S(2)}) collective-permute-start(bf16[288,128]{1,0:T(8,128)(2,1)S(1)} %collective-permute-done.7), channel_id=1, source_target_pairs={{0,1},{1,2},{2,3},{3,4},{4,5},{5,6},{6,7},{7,8},{8,9},{9,10},{10,1... | collective-permute-start | bytes 221192 | tf_op jit(solution)/shard_map/ppermute | solution.py:44
  268.0 6.3 %collective-permute-start.9 = (bf16[288,128]{1,0:T(8,128)(2,1)S(1)}, bf16[288,128]{1,0:T(8,128)(2,1)S(1)}, u32[]{:S(2)}, u32[]{:S(2)}) collective-permute-start(bf16[288,128]{1,0:T(8,128)(2,1)S(1)} %collective-permute-done.8), channel_id=1, source_target_pairs={{0,1},{1,2},{2,3},{3,4},{4,5},{5,6},{6,7},{7,8},{8,9},{9,10},{10,1... | collective-permute-start | bytes 221192 | tf_op jit(solution)/shard_map/ppermute | solution.py:44
  274.3 6.3 %collective-permute-start.10 = (bf16[288,128]{1,0:T(8,128)(2,1)S(1)}, bf16[288,128]{1,0:T(8,128)(2,1)S(1)}, u32[]{:S(2)}, u32[]{:S(2)}) collective-permute-start(bf16[288,128]{1,0:T(8,128)(2,1)S(1)} %collective-permute-done.9), channel_id=1, source_target_pairs={{0,1},{1,2},{2,3},{3,4},{4,5},{5,6},{6,7},{7,8},{8,9},{9,10},{10,1... | collective-permute-start | bytes 221192 | tf_op jit(solution)/shard_map/ppermute | solution.py:44
  280.6 6.3 %collective-permute-start.11 = (bf16[288,128]{1,0:T(8,128)(2,1)S(1)}, bf16[288,128]{1,0:T(8,128)(2,1)S(1)}, u32[]{:S(2)}, u32[]{:S(2)}) collective-permute-start(bf16[288,128]{1,0:T(8,128)(2,1)S(1)} %collective-permute-done.10), channel_id=1, source_target_pairs={{0,1},{1,2},{2,3},{3,4},{4,5},{5,6},{6,7},{7,8},{8,9},{9,10},{10,1... | collective-permute-start | bytes 221192 | tf_op jit(solution)/shard_map/ppermute | solution.py:44
  286.9 6.3 %collective-permute-start.12 = (bf16[288,128]{1,0:T(8,128)(2,1)S(1)}, bf16[288,128]{1,0:T(8,128)(2,1)S(1)}, u32[]{:S(2)}, u32[]{:S(2)}) collective-permute-start(bf16[288,128]{1,0:T(8,128)(2,1)S(1)} %collective-permute-done.11), channel_id=1, source_target_pairs={{0,1},{1,2},{2,3},{3,4},{4,5},{5,6},{6,7},{7,8},{8,9},{9,10},{10,1... | collective-permute-start | bytes 221192 | tf_op jit(solution)/shard_map/ppermute | solution.py:44
  293.2 9.0 %collective-permute-start.13 = (bf16[288,128]{1,0:T(8,128)(2,1)S(1)}, bf16[288,128]{1,0:T(8,128)(2,1)S(1)}, u32[]{:S(2)}, u32[]{:S(2)}) collective-permute-start(bf16[288,128]{1,0:T(8,128)(2,1)S(1)} %collective-permute-done.12), channel_id=1, source_target_pairs={{0,1},{1,2},{2,3},{3,4},{4,5},{5,6},{6,7},{7,8},{8,9},{9,10},{10,1... | collective-permute-start | bytes 221192 | tf_op jit(solution)/shard_map/ppermute | solution.py:44
  295.3 9.0 %copy-start.2 = (bf16[1,512]{1,0:T(2,128)(2,1)S(1)}, bf16[1,512]{1,0:T(2,128)(2,1)}, u32[]{:S(2)}) copy-start(bf16[1,512]{1,0:T(2,128)(2,1)} %param.14) | copy-start | bytes 3076
  302.2 6.3 %collective-permute-start.14 = (bf16[288,128]{1,0:T(8,128)(2,1)S(1)}, bf16[288,128]{1,0:T(8,128)(2,1)S(1)}, u32[]{:S(2)}, u32[]{:S(2)}) collective-permute-start(bf16[288,128]{1,0:T(8,128)(2,1)S(1)} %collective-permute-done.13), channel_id=1, source_target_pairs={{0,1},{1,2},{2,3},{3,4},{4,5},{5,6},{6,7},{7,8},{8,9},{9,10},{10,1... | collective-permute-start | bytes 221192 | tf_op jit(solution)/shard_map/ppermute | solution.py:44
  338.5 1.9 copy-start.3
Sparse Core Ops, SparseCore 0:
  9.4 86.7 all-gather.2
  98.3 130.1 all-gather.4
